TPU v7x, 32 devices: a whole 2x2x4 slice. The times are simulated.
32 devices in a mesh: fsdp: 16 (over z, y, x), tp: 2 (over core).
Axes of the slice: x: 2, y: 2, z: 4, core: 2. Of those that a mesh axis runs over, the one named last changes fastest.
Arguments:
- tokens: bfloat16 [4096, 896], P(('fsdp', 'tp')), may hold values from -6 to 6
- cotangent: bfloat16 [4096, 896], P(('fsdp', 'tp')), may hold values from -6 to 6
- parents: int32 [16, 2], P('fsdp'), may hold values from 0 to 0, as said below
- skip: int32 [16], P('fsdp'), may hold values 0 or 1
- w_query: bfloat16 [896, 896], P('fsdp', 'tp'), may hold values from -0.1875 to 0.1875
- key_matrix: bfloat16 [896, 128], P('fsdp', 'tp'), may hold values from -0.1875 to 0.1875
- value_matrix: bfloat16 [896, 128], P('fsdp', 'tp'), may hold values from -0.1875 to 0.1875
- w_out: bfloat16 [896, 896], P('tp', 'fsdp'), may hold values from -0.75 to 0.75
- w_gate: bfloat16 [896, 4864], P('fsdp', 'tp'), may hold values from -0.1875 to 0.1875
- w_up: bfloat16 [896, 4864], P('fsdp', 'tp'), may hold values from -0.1875 to 0.1875
- w_down: bfloat16 [4864, 896], P('tp', 'fsdp'), may hold values from -0.078125 to 0.078125
- gain_attn: bfloat16 [896], P('fsdp'), may hold values from 0.5 to 1.5
- gain_mlp: bfloat16 [896], P('fsdp'), may hold values from 0.5 to 1.5
Outputs:
- output: bfloat16 [4096, 896], P(('fsdp', 'tp'))
- grad_tokens: bfloat16 [4096, 896], P(('fsdp', 'tp'))
- grad_w_query: float32 [896, 896], P('fsdp', 'tp')
- grad_w_key: float32 [896, 128], P('fsdp', 'tp')
- grad_w_value: float32 [896, 128], P('fsdp', 'tp')
- grad_w_out: float32 [896, 896], P('tp', 'fsdp')
- grad_w_gate: float32 [896, 4864], P('fsdp', 'tp')
- grad_w_up: float32 [896, 4864], P('fsdp', 'tp')
- grad_w_down: float32 [4864, 896], P('tp', 'fsdp')
- grad_gain_attn: float32 [896], P('fsdp')
- grad_gain_mlp: float32 [896], P('fsdp')
Inputs may be any that keep to these rules, and one draw needn't show every extreme that they name: `parents`: block 0 of a tree is its own parent; each tree has two blocks, and block 1 has block 0 as its parent, so every tree's mask is causal and pos is the token's place in its tree.
All inputs are finite; a program needn't handle non-finite values. No bound on the sum of `skip` on one device may be relied on, other than what follows from the above.
Results may differ from a plain program's by a relative error of at most 0.015.
Values may be sent and summed in bfloat16 or wider, within the bound.
No kernel may reach another device: no remote copies, remote signals or barrier semaphores. Data moves between devices by JAX's collectives and lax.ppermute only.
A program may use at most 192 MiB of HBM per device.

v0:
```python
import jax
import jax.numpy as jnp
from jax import lax
from jax.sharding import PartitionSpec as P

HEAD_SIZE = 64
BLK = 128
eps = 1e-05
rotary_base = 10000.0


def cut_along(value, dim, peers):
    shape = value.shape
    pieces = value.reshape(*shape[:dim], peers, shape[dim] // peers, *shape[dim + 1 :])
    return jnp.moveaxis(pieces, dim, 0)


def summed_on_arrival(value, axis, dim):
    peers = lax.axis_size(axis)
    pieces = lax.all_to_all(cut_along(value, dim, peers), axis, 0, 0, tiled=True)
    return jnp.sum(pieces.astype(jnp.float32), axis=0)


def tree_tables(parents, blocks, block_len):
    block_ids = jnp.arange(blocks, dtype=jnp.int32)
    ancestry = jnp.eye(blocks, dtype=jnp.float32)
    depths = jnp.zeros((blocks,), jnp.float32)
    picked = (block_ids == parents[1]).astype(jnp.float32)
    inherited = jnp.sum(picked[:, None] * ancestry, axis=0)
    ancestry = ancestry.at[1].set(jnp.maximum(ancestry[1], inherited))
    depths = depths.at[1].set(jnp.sum(picked * depths) + 1.0)
    token_ids = jnp.arange(blocks * block_len, dtype=jnp.int32)
    spread = jnp.repeat(jnp.repeat(ancestry, block_len, axis=0), block_len, axis=1)
    visible = (spread > 0.5) & (token_ids[None, :] <= token_ids[:, None])
    token_position = jnp.repeat(depths, block_len) * block_len + (token_ids % block_len).astype(
        jnp.float32
    )
    return (visible, token_position)


def apply_rotation(values, token_position, head_count, direction):
    count_of_rows = values.shape[0]
    shaped = values.reshape(count_of_rows, head_count, HEAD_SIZE)
    half_size = HEAD_SIZE // 2
    frequency = rotary_base ** (-2.0 * jnp.arange(half_size, dtype=jnp.float32) / HEAD_SIZE)
    angles = token_position[:, None] * frequency[None, :]
    cosine = jnp.cos(angles)[:, None, :]
    sine_part = direction * jnp.sin(angles)[:, None, :]
    first_half = shaped[..., :half_size]
    second_half = shaped[..., half_size:]
    turned = jnp.concatenate(
        [
            first_half * cosine - second_half * sine_part,
            second_half * cosine + first_half * sine_part,
        ],
        axis=-1,
    )
    return turned.reshape(count_of_rows, head_count * HEAD_SIZE)


def fetch_attention(w_query, key_matrix, value_matrix, w_out, gain_attn):
    return (
        lax.all_gather(w_query, "fsdp", axis=0, tiled=True),
        lax.all_gather(key_matrix, "fsdp", axis=0, tiled=True),
        lax.all_gather(value_matrix, "fsdp", axis=0, tiled=True),
        lax.all_gather(w_out, "fsdp", axis=1, tiled=True),
        lax.all_gather(gain_attn, "fsdp", axis=0, tiled=True),
    )


def fetch_mlp(w_gate, w_up, w_down, gain_mlp):
    return (
        lax.all_gather(w_gate, "fsdp", axis=0, tiled=True),
        lax.all_gather(w_up, "fsdp", axis=0, tiled=True),
        lax.all_gather(w_down, "fsdp", axis=1, tiled=True),
        lax.all_gather(gain_mlp, "fsdp", axis=0, tiled=True),
    )


def rows_inner(first_array, second_array):
    return lax.dot_general(
        first_array, second_array, (((0,), (0,)), ((), ())), preferred_element_type=jnp.float32
    )


def against(first_array, second_array):
    return lax.dot_general(
        first_array, second_array, (((1,), (1,)), ((), ())), preferred_element_type=jnp.float32
    )


def norm_back(grad_normed, scaled, statistic, gain_vector):
    grad_scaled = grad_normed * gain_vector
    return statistic * (
        grad_scaled - scaled * jnp.mean(grad_scaled * scaled, axis=-1, keepdims=True)
    )


def on_device(
    tokens,
    cotangent,
    parents,
    skip,
    w_query,
    key_matrix,
    value_matrix,
    w_out,
    w_gate,
    w_up,
    w_down,
    gain_attn,
    gain_mlp,
):
    half_rows = tokens.shape[0]
    seq_len = half_rows * lax.axis_size("tp")
    blocks = seq_len // BLK
    shard_rows = w_query.shape[0]
    heads_here = w_query.shape[1] // HEAD_SIZE
    kv_here = key_matrix.shape[1] // HEAD_SIZE
    heads_per_group = heads_here // kv_here
    query_cols = heads_here * HEAD_SIZE
    kv_cols = kv_here * HEAD_SIZE
    ff_here = w_gate.shape[1]
    score_scale = HEAD_SIZE ** (-0.5)
    visible, token_position = tree_tables(parents[0], blocks, BLK)
    active = (1 - skip[0]).astype(jnp.float32)
    query_all, key_all, value_all, out_all, gain_one = fetch_attention(
        w_query, key_matrix, value_matrix, w_out, gain_attn
    )
    inputs = tokens.astype(jnp.float32)
    stat_one = lax.rsqrt(jnp.mean(inputs * inputs, axis=-1, keepdims=True) + eps)
    scaled_one = inputs * stat_one
    gain_one_wide = gain_one.astype(jnp.float32)
    normed_input = (scaled_one * gain_one_wide).astype(jnp.bfloat16)
    normed_all = lax.all_gather(normed_input, "tp", axis=0, tiled=True)
    query_rows = apply_rotation(
        jnp.dot(normed_all, query_all, preferred_element_type=jnp.float32),
        token_position,
        heads_here,
        1.0,
    ).astype(jnp.bfloat16)
    key_row_block = apply_rotation(
        jnp.dot(normed_all, key_all, preferred_element_type=jnp.float32),
        token_position,
        kv_here,
        1.0,
    ).astype(jnp.bfloat16)
    value_row_block = jnp.dot(normed_all, value_all, preferred_element_type=jnp.float32).astype(
        jnp.bfloat16
    )
    query_per_head = query_rows.reshape(seq_len, kv_here, heads_per_group, HEAD_SIZE)
    key_per_head = key_row_block.reshape(seq_len, kv_here, HEAD_SIZE)
    value_per_head = value_row_block.reshape(seq_len, kv_here, HEAD_SIZE)

    def score_table():
        raw_scores = (
            jnp.einsum(
                "qhgd,khd->hgqk", query_per_head, key_per_head, preferred_element_type=jnp.float32
            )
            * score_scale
        )
        return jnp.where(visible, raw_scores, -1e30)

    scores = score_table()
    row_max = jnp.max(scores, axis=-1, keepdims=True)
    exponent = jnp.exp(scores - row_max)
    row_total = jnp.sum(exponent, axis=-1, keepdims=True)
    log_total = row_max + jnp.log(row_total)
    probs_low = (exponent / row_total).astype(jnp.bfloat16)
    attended = jnp.einsum(
        "hgqk,khd->qhgd", probs_low, value_per_head, preferred_element_type=jnp.float32
    )
    attended = attended.reshape(seq_len, query_cols).astype(jnp.bfloat16)
    branch = lax.psum_scatter(
        jnp.dot(attended, out_all, preferred_element_type=jnp.float32).astype(jnp.bfloat16),
        "tp",
        scatter_dimension=0,
        tiled=True,
    ).astype(jnp.float32)
    middle = inputs + active * branch
    gate_all, up_all, down_all, gain_two = fetch_mlp(w_gate, w_up, w_down, gain_mlp)
    stat_two = lax.rsqrt(jnp.mean(middle * middle, axis=-1, keepdims=True) + eps)
    scaled_two = middle * stat_two
    gain_two_wide = gain_two.astype(jnp.float32)
    normed_mlp = (scaled_two * gain_two_wide).astype(jnp.bfloat16)
    normed_mlp_all = lax.all_gather(normed_mlp, "tp", axis=0, tiled=True)
    gate_sum = jnp.dot(normed_mlp_all, gate_all, preferred_element_type=jnp.float32)
    upward = jnp.dot(normed_mlp_all, up_all, preferred_element_type=jnp.float32)
    sigmoid_gate = jax.nn.sigmoid(gate_sum)
    hidden = (gate_sum * sigmoid_gate * upward).astype(jnp.bfloat16)
    mlp_result = lax.psum_scatter(
        jnp.dot(hidden, down_all, preferred_element_type=jnp.float32).astype(jnp.bfloat16),
        "tp",
        scatter_dimension=0,
        tiled=True,
    ).astype(jnp.float32)
    output = (middle + active * mlp_result).astype(jnp.bfloat16)
    grad_out = cotangent.astype(jnp.float32)
    grad_mlp = (active * grad_out).astype(jnp.bfloat16)
    grad_mlp_all = lax.all_gather(grad_mlp, "tp", axis=0, tiled=True)
    gate_all, up_all, down_all, gain_two = fetch_mlp(w_gate, w_up, w_down, gain_mlp)
    gain_two_wide = gain_two.astype(jnp.float32)
    grad_hidden = against(grad_mlp_all, down_all)
    grad_gate = (
        grad_hidden * upward * sigmoid_gate * (1.0 + gate_sum * (1.0 - sigmoid_gate))
    ).astype(jnp.bfloat16)
    grad_up = (grad_hidden * gate_sum * sigmoid_gate).astype(jnp.bfloat16)
    grad_normed_mlp = lax.psum_scatter(
        (against(grad_gate, gate_all) + against(grad_up, up_all)).astype(jnp.bfloat16),
        "tp",
        scatter_dimension=0,
        tiled=True,
    ).astype(jnp.float32)
    column_part = normed_mlp_all
    grad_part = grad_mlp_all
    mlp_grads = lax.psum_scatter(
        jnp.concatenate(
            [
                rows_inner(column_part, grad_gate),
                rows_inner(column_part, grad_up),
                rows_inner(grad_part, hidden),
            ],
            axis=1,
        ),
        "fsdp",
        scatter_dimension=0,
        tiled=True,
    )
    grad_gain_two = jnp.sum(grad_normed_mlp * scaled_two, axis=0)
    grad_middle = grad_out + norm_back(grad_normed_mlp, scaled_two, stat_two, gain_two_wide)
    grad_branch = (active * grad_middle).astype(jnp.bfloat16)
    grad_branch_all = lax.all_gather(grad_branch, "tp", axis=0, tiled=True)
    query_all, key_all, value_all, out_all, gain_one = fetch_attention(
        w_query, key_matrix, value_matrix, w_out, gain_attn
    )
    gain_one_wide = gain_one.astype(jnp.float32)
    grad_attended = (
        against(grad_branch_all, out_all)
        .astype(jnp.bfloat16)
        .reshape(seq_len, kv_here, heads_per_group, HEAD_SIZE)
    )
    probs = jnp.exp(score_table() - log_total)
    probs_low = probs.astype(jnp.bfloat16)
    grad_probs = jnp.einsum(
        "qhgd,khd->hgqk", grad_attended, value_per_head, preferred_element_type=jnp.float32
    )
    grad_value = jnp.einsum(
        "hgqk,qhgd->khd", probs_low, grad_attended, preferred_element_type=jnp.float32
    )
    grad_value = grad_value.reshape(seq_len, kv_cols).astype(jnp.bfloat16)
    grad_scores = (
        probs * (grad_probs - jnp.sum(probs * grad_probs, axis=-1, keepdims=True))
    ).astype(jnp.bfloat16)
    grad_query = (
        jnp.einsum(
            "hgqk,khd->qhgd", grad_scores, key_per_head, preferred_element_type=jnp.float32
        ).reshape(seq_len, query_cols)
        * score_scale
    )
    grad_key = (
        jnp.einsum(
            "hgqk,qhgd->khd", grad_scores, query_per_head, preferred_element_type=jnp.float32
        ).reshape(seq_len, kv_cols)
        * score_scale
    )
    grad_query = apply_rotation(grad_query, token_position, heads_here, -1.0).astype(jnp.bfloat16)
    grad_key = apply_rotation(grad_key, token_position, kv_here, -1.0).astype(jnp.bfloat16)
    first_term = against(grad_query, query_all)
    second_term = against(grad_key, key_all)
    third_term = against(grad_value, value_all)
    grad_normed = lax.psum_scatter(
        (first_term + second_term + third_term).astype(jnp.bfloat16),
        "tp",
        scatter_dimension=0,
        tiled=True,
    ).astype(jnp.float32)
    column_part = normed_all
    grad_part = grad_branch_all
    attn_grads = summed_on_arrival(
        jnp.concatenate(
            [
                rows_inner(column_part, grad_query),
                rows_inner(column_part, grad_key),
                rows_inner(column_part, grad_value),
                rows_inner(grad_part, attended),
            ],
            axis=1,
        ).astype(jnp.bfloat16),
        "fsdp",
        0,
    )
    grad_gain_one = jnp.sum(grad_normed * scaled_one, axis=0)
    grad_tokens = (
        grad_middle + norm_back(grad_normed, scaled_one, stat_one, gain_one_wide)
    ).astype(jnp.bfloat16)
    gain_total_one, gain_total_two = lax.psum((grad_gain_one, grad_gain_two), ("fsdp", "tp"))
    offset = lax.axis_index("fsdp") * shard_rows
    grad_gain_attn = lax.dynamic_slice_in_dim(gain_total_one, offset, shard_rows)
    grad_gain_mlp = lax.dynamic_slice_in_dim(gain_total_two, offset, shard_rows)
    grad_w_query = attn_grads[:, :query_cols]
    grad_w_key = attn_grads[:, query_cols : query_cols + kv_cols]
    grad_w_value = attn_grads[:, query_cols + kv_cols : query_cols + 2 * kv_cols]
    grad_w_out = attn_grads[:, query_cols + 2 * kv_cols :].T
    grad_w_gate = mlp_grads[:, :ff_here]
    grad_w_up = mlp_grads[:, ff_here : 2 * ff_here]
    grad_w_down = mlp_grads[:, 2 * ff_here :].T
    return (
        output,
        grad_tokens,
        grad_w_query,
        grad_w_key,
        grad_w_value,
        grad_w_out,
        grad_w_gate,
        grad_w_up,
        grad_w_down,
        grad_gain_attn,
        grad_gain_mlp,
    )


def solution(mesh):
    in_specs = (
        P(("fsdp", "tp"), None),
        P(("fsdp", "tp"), None),
        P("fsdp", None),
        P("fsdp"),
        P("fsdp", "tp"),
        P("fsdp", "tp"),
        P("fsdp", "tp"),
        P("tp", "fsdp"),
        P("fsdp", "tp"),
        P("fsdp", "tp"),
        P("tp", "fsdp"),
        P("fsdp"),
        P("fsdp"),
    )
    out_specs = (
        P(("fsdp", "tp"), None),
        P(("fsdp", "tp"), None),
        P("fsdp", "tp"),
        P("fsdp", "tp"),
        P("fsdp", "tp"),
        P("tp", "fsdp"),
        P("fsdp", "tp"),
        P("fsdp", "tp"),
        P("tp", "fsdp"),
        P("fsdp"),
        P("fsdp"),
    )
    return jax.shard_map(
        on_device, mesh=mesh, in_specs=in_specs, out_specs=out_specs, check_vma=False
    )
```

profile of v0, /device:TPU:0, one launch (start us, length us, event | category | flops | bytes accessed | tf_op | source)
XLA Modules:
  0.0 1254.3 jit_solution(5714153399740913930)
XLA Ops:
  8.1 1.2 slice.77
  10.1 1.1 fusion.34
  11.5 1.3 fusion.70
  13.4 0.8 dynamic-update-slice.6
  14.3 0.8 dynamic-update-slice.5
  15.1 44.2 %all-reduce.4 = (bf16[896]{0:T(1024)(128)(2,1)}, bf16[896]{0:T(1024)(128)(2,1)S(1)}) all-reduce(bf16[896]{0:T(1024)(128)(2,1)S(1)} %dynamic-update-slice.6, bf16[896]{0:T(1024)(128)(2,1)S(1)} %dynamic-update-slice.5), channel_id=1, replica_groups=mesh['fsdp'=16,'tp'=2] {'fsdp'}, use_global_device_ids=true, to_apply=%add.1 | all-reduce | flops 1792 | bytes 7168
  59.4 37.0 %all_gather.51 = bf16[896,64]{1,0:T(8,128)(2,1)S(1)} all-gather(bf16[56,64]{1,0:T(8,128)(2,1)} %param.22), channel_id=1, replica_groups=mesh['fsdp'=16,'tp'=2] {'fsdp'}, dimensions={0}, use_global_device_ids=true | all-gather | bytes 121856 | tf_op jit(solution)/shard_map/all_gather | solution.py:64
  96.4 38.9 %all_gather.50 = bf16[896,64]{1,0:T(8,128)(2,1)S(1)} all-gather(bf16[56,64]{1,0:T(8,128)(2,1)} %param.23), channel_id=1, replica_groups=mesh['fsdp'=16,'tp'=2] {'fsdp'}, dimensions={0}, use_global_device_ids=true | all-gather | bytes 121856 | tf_op jit(solution)/shard_map/all_gather | solution.py:65
  135.3 1.1 fusion.31
  136.5 2.1 all_gather.49
  139.2 0.8 broadcast_multiply_fusion
  140.3 40.7 %all_gather.52 = bf16[896,448]{1,0:T(8,128)(2,1)S(1)} all-gather(bf16[56,448]{1,0:T(8,128)(2,1)S(1)} %copy-done.37), channel_id=1, replica_groups=mesh['fsdp'=16,'tp'=2] {'fsdp'}, dimensions={0}, use_global_device_ids=true | all-gather | bytes 852992 | tf_op jit(solution)/shard_map/all_gather | solution.py:63
  181.5 43.4 %all_gather.53 = bf16[448,896]{0,1:T(8,128)(2,1)S(1)} all-gather(bf16[448,56]{0,1:T(8,128)(2,1)S(1)} %copy-done.38), channel_id=1, replica_groups=mesh['fsdp'=16,'tp'=2] {'fsdp'}, dimensions={1}, use_global_device_ids=true | all-gather | bytes 852992 | tf_op jit(solution)/shard_map/all_gather | solution.py:66
  226.4 0.7 copy-done.18
  227.1 1.2 convolution_convert_fusion.3
  230.8 1.3 convert_element_type.213
  232.1 1.0 fusion.29
  233.1 2.3 all_gather.59
  235.3 1.3 log_add_fusion
  236.7 1.1 multiply_reduce_fusion
  238.4 1.1 multiply_convert_fusion.4
  239.4 2.3 all_gather.55
  241.7 63.3 %all-gather.6.cloned.1.call-done = bf16[896,2432]{1,0:T(8,128)(2,1)} async-done(((bf16[56,2432]{1,0:T(8,128)(2,1)}), bf16[896,2432]{1,0:T(8,128)(2,1)}) %all-gather.6.cloned.1.call-update) | async-done | bytes 4358160 | tf_op jit(solution)/shard_map/all_gather | solution.py:74
  305.1 5.3 fusion.74
  310.4 73.4 %all-gather.4.cloned.1.call-done = bf16[896,2432]{1,0:T(8,128)(2,1)} async-done(((bf16[56,2432]{1,0:T(8,128)(2,1)}), bf16[896,2432]{1,0:T(8,128)(2,1)}) %all-gather.4.cloned.1.call-update) | async-done | bytes 4358160 | tf_op jit(solution)/shard_map/all_gather | solution.py:73
  383.7 5.3 fusion.73
  389.1 73.4 %all-gather.8.cloned.1.call-done = bf16[2432,896]{0,1:T(8,128)(2,1)} async-done(((bf16[2432,56]{0,1:T(8,128)(2,1)}), bf16[2432,896]{0,1:T(8,128)(2,1)}) %all-gather.8.cloned.1.call-update) | async-done | bytes 4358160 | tf_op jit(solution)/shard_map/all_gather | solution.py:75
  462.4 6.9 multiply_convert_fusion
  469.3 1.5 fusion.75
  470.9 4.6 fusion.6
  475.7 6.3 fusion.78
  482.0 4.8 fusion.77
  486.9 2.0 fusion.30
  488.9 1.4 multiply_convert_fusion.3
  490.3 2.1 all_gather.60
  496.9 1.1 fusion.5
  498.1 4.6 convolution_convert_fusion.2
  502.7 4.8 fusion.79
  507.6 19.7 %pad_maximum_fusion = f32[896,7296]{1,0:T(8,128)} fusion(f32[896,2432]{1,0:T(8,128)} %fusion.79, f32[896,2432]{1,0:T(8,128)} %fusion.78, f32[896,2432]{1,0:T(8,128)} %fusion.77), kind=kLoop, calls=%fused_computation | loop fusion | flops 13074432 | bytes 52297728 | tf_op jit(solution)/shard_map/concatenate | solution.py:217
  527.5 0.8 copy-done.6
  529.9 2.1 pad_maximum_fusion.1
  532.0 4.4 all-to-all-start
  537.2 1.2 fusion.33
  538.4 106.9 %all-reduce.3 = (f32[896]{0:T(1024)S(1)}, f32[896]{0:T(1024)S(1)}) all-reduce(f32[896]{0:T(1024)S(1)} %get-tuple-element.37, f32[896]{0:T(1024)S(1)} %copy-done.41), channel_id=1, replica_groups=mesh['fsdp'=16,'tp'=2] {'fsdp','tp'}, use_global_device_ids=true, to_apply=%region_15.16 | all-reduce | flops 1792 | bytes 14336 | tf_op jit(solution)/shard_map/psum | solution.py:296
  646.6 2.2 fusion.26
  649.8 0.7 slice_bitcast_fusion
  650.5 593.5 %all-reduce.7.cloned.1.call-done = f32[896,7296]{1,0:T(8,128)} async-done(((f32[896,7296]{1,0:T(8,128)}), f32[896,7296]{1,0:T(8,128)}) %all-reduce.7.cloned.1.call-update) | async-done | bytes 26148880
  1244.0 2.9 dynamic-slice_bitcast_fusion
  (173 shorter events, 14.8 us)
Async XLA Ops:
  8.0 228.6 %reduce-scatter.5.cloned.1.call-start = ((), (), s32[]{:S(2)}) async-start(), calls=%async_computation.5 | async-start | bytes 688128 | tf_op jit(solution)/shard_map/reduce_scatter | solution.py:174
  8.1 131.9 %copy-start.46 = (f32[32]{0:T(128)}, f32[32]{0:T(128)S(1)}, u32[]{:S(2)}) copy-start(f32[32]{0:T(128)S(1)} %multiply_power_fusion) | copy-start | bytes 388
  8.1 131.9 %copy-start.42 = (f32[256]{0:T(256)}, f32[256]{0:T(256)S(1)}, u32[]{:S(2)}) copy-start(f32[256]{0:T(256)S(1)} %fusion.62) | copy-start | bytes 3076
  10.1 130.1 %copy-start.37 = (bf16[56,448]{1,0:T(8,128)(2,1)S(1)}, bf16[56,448]{1,0:T(8,128)(2,1)}, u32[]{:S(2)}) copy-start(bf16[56,448]{1,0:T(8,128)(2,1)} %param.21) | copy-start | bytes 150532
  11.2 124.1 %copy-start.48 = (f32[128]{0:T(128)}, f32[128]{0:T(128)S(1)}, u32[]{:S(2)}) copy-start(f32[128]{0:T(128)S(1)} %add_rsqrt_fusion.1) | copy-start | bytes 1540
  59.3 76.0 %copy-start.31 = (f32[896]{0:T(1024)}, f32[896]{0:T(1024)S(1)}, u32[]{:S(2)}) copy-start(f32[896]{0:T(1024)S(1)} %convert_element_type.200) | copy-start | bytes 10756
  96.4 43.6 %copy-start.12 = (bf16[896,64]{1,0:T(8,128)(2,1)}, bf16[896,64]{1,0:T(8,128)(2,1)S(1)}, u32[]{:S(2)}) copy-start(bf16[896,64]{1,0:T(8,128)(2,1)S(1)} %all_gather.51) | copy-start | bytes 344068
  135.3 45.7 %copy-start.10 = (bf16[896,64]{1,0:T(8,128)(2,1)}, bf16[896,64]{1,0:T(8,128)(2,1)S(1)}, u32[]{:S(2)}) copy-start(bf16[896,64]{1,0:T(8,128)(2,1)S(1)} %all_gather.50) | copy-start | bytes 344068
  138.9 86.9 %copy-start.27 = (bf16[256,64,1]{0,1,2:T(8,128)(2,1)}, bf16[256,64,1]{0,1,2:T(8,128)(2,1)S(1)}, u32[]{:S(2)}) copy-start(bf16[256,64,1]{0,1,2:T(8,128)(2,1)S(1)} %fusion.11) | copy-start | bytes 98308
  138.9 42.6 %copy-start.38 = (bf16[448,56]{0,1:T(8,128)(2,1)S(1)}, bf16[448,56]{0,1:T(8,128)(2,1)}, u32[]{:S(2)}) copy-start(bf16[448,56]{0,1:T(8,128)(2,1)} %param.24) | copy-start | bytes 150532
  140.0 84.9 %copy-start.24 = (f32[256,32]{0,1:T(8,128)}, f32[256,32]{0,1:T(8,128)S(1)}, u32[]{:S(2)}) copy-start(f32[256,32]{0,1:T(8,128)S(1)} %get-tuple-element.65) | copy-start | bytes 98308
  140.2 84.7 %copy-start.33 = (bf16[256,32]{0,1:T(8,128)(2,1)}, bf16[256,32]{0,1:T(8,128)(2,1)S(1)}, u32[]{:S(2)}) copy-start(bf16[256,32]{0,1:T(8,128)(2,1)S(1)} %get-tuple-element.61) | copy-start | bytes 49156
  140.2 84.7 %copy-start.35 = (bf16[256,32]{0,1:T(8,128)(2,1)}, bf16[256,32]{0,1:T(8,128)(2,1)S(1)}, u32[]{:S(2)}) copy-start(bf16[256,32]{0,1:T(8,128)(2,1)S(1)} %get-tuple-element.62) | copy-start | bytes 49156
  224.9 1.5 copy-start.1
  227.1 9.6 copy-start
  228.3 76.7 %all-gather.6.cloned.1.call-start = ((), (), s32[]{:S(2)}) async-start(), calls=%async_computation.7 | async-start | bytes 4630528 | tf_op jit(solution)/shard_map/all_gather | solution.py:74
  228.9 154.8 %all-gather.4.cloned.1.call-start = ((), (), s32[]{:S(2)}) async-start(), calls=%async_computation.6 | async-start | bytes 4630528 | tf_op jit(solution)/shard_map/all_gather | solution.py:73
  229.5 232.9 %all-gather.8.cloned.1.call-start = ((), (), s32[]{:S(2)}) async-start(), calls=%async_computation.8 | async-start | bytes 4630528 | tf_op jit(solution)/shard_map/all_gather | solution.py:75
  230.1 256.8 %reduce-scatter.9.cloned.1.call-start = ((), (), s32[]{:S(2)}) async-start(), calls=%async_computation.10 | async-start | bytes 688128 | tf_op jit(solution)/shard_map/reduce_scatter | solution.py:208
  462.4 6.9 copy-start.52
  469.3 1.6 copy-start.15
  469.3 1.6 copy-start.17
  475.5 61.7 %reduce-scatter.11.cloned.1.call-start = ((), (), s32[]{:S(2)}) async-start(), calls=%async_computation.11 | async-start | bytes 688128 | tf_op jit(solution)/shard_map/reduce_scatter | solution.py:271
  475.7 6.3 copy-start.3
  475.7 6.3 copy-start.16
  486.9 5.6 copy-start.2
  488.9 4.1 copy-start.26
  488.9 1.4 copy-start.50
  493.4 3.4 copy-start.22
  493.9 1.3 copy-start.34
  493.9 1.3 copy-start.36
  496.5 1.5 copy-start.14
  498.0 148.5 %reduce-scatter.7.cloned.1.call-start = ((), (), s32[]{:S(2)}) async-start(), calls=%async_computation.9 | async-start | bytes 688128 | tf_op jit(solution)/shard_map/reduce_scatter | solution.py:191
  498.1 4.6 copy-start.7
  507.5 736.5 %all-reduce.7.cloned.1.call-start = ((), (), s32[]{:S(2)}) async-start(), calls=%async_computation.12 | async-start | bytes 52297728
  527.3 1.0 copy-start.6
  527.3 1.5 copy-start.23
  528.3 1.2 copy-start.19
  532.0 5.2 copy-start.32
  532.0 5.2 copy-start.49
  532.0 6.4 copy-start.41
  532.0 114.5 %copy-start.4 = (bf16[128,896]{1,0:T(8,128)(2,1)S(1)}, bf16[128,896]{1,0:T(8,128)(2,1)}, u32[]{:S(2)}) copy-start(bf16[128,896]{1,0:T(8,128)(2,1)} %reduce-scatter.5.cloned.1.call-done) | copy-start | bytes 688132
  532.0 114.5 %copy-start.8 = (bf16[128,896]{1,0:T(8,128)(2,1)S(1)}, bf16[128,896]{1,0:T(8,128)(2,1)}, u32[]{:S(2)}) copy-start(bf16[128,896]{1,0:T(8,128)(2,1)} %param.18) | copy-start | bytes 688132
  532.0 114.5 %copy-start.9 = (bf16[128,896]{1,0:T(8,128)(2,1)S(1)}, bf16[128,896]{1,0:T(8,128)(2,1)}, u32[]{:S(2)}) copy-start(bf16[128,896]{1,0:T(8,128)(2,1)} %reduce-scatter.9.cloned.1.call-done) | copy-start | bytes 688132
  532.0 114.5 %copy-start.30 = (f32[896]{0:T(1024)S(1)}, f32[896]{0:T(1024)}, u32[]{:S(2)}) copy-start(f32[896]{0:T(1024)} %convert_element_type.213) | copy-start | bytes 10756
  532.0 114.5 %copy-start.45 = (f32[128]{0:T(128)S(1)}, f32[128]{0:T(128)}, u32[]{:S(2)}) copy-start(f32[128]{0:T(128)} %copy-done.44) | copy-start | bytes 1540
  532.0 114.5 %copy-start.51 = (f32[128]{0:T(128)S(1)}, f32[128]{0:T(128)}, u32[]{:S(2)}) copy-start(f32[128]{0:T(128)} %copy-done.50) | copy-start | bytes 1540
  532.0 116.7 %all-to-all-start = ((bf16[16,56,1024]{2,1,0:T(8,128)(2,1)}), bf16[16,56,1024]{2,1,0:T(8,128)(2,1)S(1)}, u32[]{:S(2)}, u32[]{:S(2)}) async-start(bf16[16,56,1024]{2,1,0:T(8,128)(2,1)} %pad_maximum_fusion.1), calls=%async_computation.4 | async-start | bytes 3670016 | tf_op jit(solution)/shard_map/all_to_all | solution.py:20
  (14 other events, 11.7 us)
Sparse Core Ops, SparseCore 0:
  228.5 3.9 reduce-scatter.4
  475.6 6.4 reduce-scatter.8
  498.1 6.5 reduce-scatter.10
  507.6 8.8 reduce-scatter.6
Sparse Core Ops, SparseCore 1:
  231.9 73.1 all-gather.5
  308.0 75.7 all-gather.3
  386.7 75.7 all-gather.7
  527.4 716.6 all-reduce.6
where the time goes:
time: 1260 us; the launch traced here: 1250 us
  waiting for transfers between devices  805 us (64%)
  blocking collectives  320 us (25%)
  matrix products  52.7 us (4%)
  other arithmetic  39.9 us (3%)
  between operations  18.2 us (1%)
  local copies, waits for them, and re-layouts  13.3 us (1%)
    unnamed x9, waiting for transfers between devices  595 us
    psum x1, blocking collectives, on_device(): lax.psum((grad_gain_one, grad_gain_two), ('fsdp', 'tp'))  107 us
    all_gather x1, waiting for transfers between devices, fetch_mlp(): lax.all_gather(w_gate, 'fsdp', axis=0, tiled=True)  73.4 us
    all_gather x1, waiting for transfers between devices, fetch_mlp(): lax.all_gather(w_down, 'fsdp', axis=1, tiled=True)  73.4 us
    all_gather x1, waiting for transfers between devices, fetch_mlp(): lax.all_gather(w_up, 'fsdp', axis=0, tiled=True)  63.3 us
    unnamed x1, blocking collectives  44.2 us
    all_gather x1, blocking collectives, fetch_attention(): lax.all_gather(w_out, 'fsdp', axis=1, tiled=True)  43.4 us
    all_gather x1, blocking collectives, fetch_attention(): lax.all_gather(w_query, 'fsdp', axis=0, tiled=True)  40.7 us
  transfers between devices with their start and end apart: 9, of which 4 were waited for; matrix products, arithmetic and copies ran while one was open for 5% of the time, Pallas kernels for 0%

commit v1 on v0

--- a/solution.py
+++ b/solution.py
@@ -7,6 +7,27 @@
 BLK = 128
 eps = 1e-05
 rotary_base = 10000.0
+
+
+def collect(value, axis, dim):
+    length, index, rows = (lax.axis_size(axis), lax.axis_index(axis), value.shape[dim])
+    forward = [(i, (i + 1) % length) for i in range(length)]
+    backward = [(i, (i - 1) % length) for i in range(length)]
+    out = jnp.zeros((*value.shape[:dim], length * rows, *value.shape[dim + 1 :]), value.dtype)
+    out = lax.dynamic_update_slice_in_dim(out, value, index * rows, axis=dim)
+    from_left = from_right = value
+    half = length // 2
+    for turn in range(1, half + 1):
+        from_left = lax.ppermute(from_left, axis, forward)
+        out = lax.dynamic_update_slice_in_dim(
+            out, from_left, (index - turn) % length * rows, axis=dim
+        )
+        if turn < length - half:
+            from_right = lax.ppermute(from_right, axis, backward)
+            out = lax.dynamic_update_slice_in_dim(
+                out, from_right, (index + turn) % length * rows, axis=dim
+            )
+    return out
 
 
 def cut_along(value, dim, peers):
@@ -60,7 +81,7 @@
 
 def fetch_attention(w_query, key_matrix, value_matrix, w_out, gain_attn):
     return (
-        lax.all_gather(w_query, "fsdp", axis=0, tiled=True),
+        collect(w_query, "fsdp", 0),
         lax.all_gather(key_matrix, "fsdp", axis=0, tiled=True),
         lax.all_gather(value_matrix, "fsdp", axis=0, tiled=True),
         lax.all_gather(w_out, "fsdp", axis=1, tiled=True),

time: 1260 us -> 1280 us (1.016)
  blocking collectives: 320 us -> 276 us
  starting transfers between devices: 4.91 us -> 44.2 us
  waiting for transfers between devices: 805 us -> 830 us
    all_gather x1 -> x0, blocking collectives: 40.7 us -> none  [fetch_attention(): lax.all_gather(w_query, 'fsdp', axis=0, tiled=True)]
    ppermute x0 -> x15, starting transfers between devices: none -> 39.4 us  [the longest x7 39.4 us: collect(): from_right = lax.ppermute(from_right, axis, backward)]
    ppermute x0 -> x15, waiting for transfers between devices: none -> 25.3 us  [the longest x8 16.8 us: collect(): from_left = lax.ppermute(from_left, axis, forward)]
  transfers between devices with their start and end apart: 9 -> 24, of which waited for: 4 -> 15; matrix products, arithmetic and copies ran while one was open for 5% -> 6% of each run, Pallas kernels for 0% -> 0%
where the time goes in v1:
time: 1280 us
  waiting for transfers between devices  830 us (65%)
  blocking collectives  276 us (22%)
  matrix products  55 us (4%)
  starting transfers between devices  44.2 us (3%)
  other arithmetic  41.1 us (3%)
  between operations  18.5 us (1%)
  local copies, waits for them, and re-layouts  14 us (1%)
    unnamed x9, waiting for transfers between devices  595 us
    psum x1, blocking collectives, on_device(): lax.psum((grad_gain_one, grad_gain_two), ('fsdp', 'tp'))  107 us
    all_gather x1, waiting for transfers between devices, fetch_mlp(): lax.all_gather(w_down, 'fsdp', axis=1, tiled=True)  73.4 us
    all_gather x1, waiting for transfers between devices, fetch_mlp(): lax.all_gather(w_gate, 'fsdp', axis=0, tiled=True)  73.3 us
    all_gather x1, waiting for transfers between devices, fetch_mlp(): lax.all_gather(w_up, 'fsdp', axis=0, tiled=True)  63 us
    unnamed x1, blocking collectives  42.8 us
    all_gather x1, blocking collectives, fetch_attention(): lax.all_gather(w_out, 'fsdp', axis=1, tiled=True)  40.9 us
    ppermute x7, starting transfers between devices, collect(): from_right = lax.ppermute(from_right, axis, backward)  39.4 us
  transfers between devices with their start and end apart: 24, of which 15 were waited for; matrix products, arithmetic and copies ran while one was open for 6% of the time, Pallas kernels for 0%

profile of v1, /device:TPU:0, one launch (start us, length us, event | category | flops | bytes accessed | tf_op | source)
XLA Modules:
  0.0 1278.7 jit_solution(391905807095752740)
XLA Ops:
  8.1 7.0 collective-permute-start.1
  18.4 1.3 fusion.73
  22.1 42.8 %all-reduce.4 = (bf16[896]{0:T(1024)(128)(2,1)}, bf16[896]{0:T(1024)(128)(2,1)S(1)}) all-reduce(bf16[896]{0:T(1024)(128)(2,1)S(1)} %dynamic-update-slice.6, bf16[896]{0:T(1024)(128)(2,1)S(1)} %dynamic-update-slice.5), channel_id=1, replica_groups=mesh['fsdp'=16,'tp'=2] {'fsdp'}, use_global_device_ids=true, to_apply=%add.1 | all-reduce | flops 1792 | bytes 7168
  64.9 37.0 %all_gather.47 = bf16[896,64]{1,0:T(8,128)(2,1)S(1)} all-gather(bf16[56,64]{1,0:T(8,128)(2,1)} %param.22), channel_id=1, replica_groups=mesh['fsdp'=16,'tp'=2] {'fsdp'}, dimensions={0}, use_global_device_ids=true | all-gather | bytes 121856 | tf_op jit(solution)/shard_map/all_gather | solution.py:85
  101.9 38.9 %all_gather.46 = bf16[896,64]{1,0:T(8,128)(2,1)S(1)} all-gather(bf16[56,64]{1,0:T(8,128)(2,1)} %param.23), channel_id=1, replica_groups=mesh['fsdp'=16,'tp'=2] {'fsdp'}, dimensions={0}, use_global_device_ids=true | all-gather | bytes 121856 | tf_op jit(solution)/shard_map/all_gather | solution.py:86
  141.9 2.1 all_gather.45
  146.9 40.9 %all_gather.48 = bf16[448,896]{0,1:T(8,128)(2,1)S(1)} all-gather(bf16[448,56]{0,1:T(8,128)(2,1)S(1)} %copy-done.36), channel_id=1, replica_groups=mesh['fsdp'=16,'tp'=2] {'fsdp'}, dimensions={1}, use_global_device_ids=true | all-gather | bytes 852992 | tf_op jit(solution)/shard_map/all_gather | solution.py:87
  188.8 2.9 collective-permute-start.3
  191.7 2.0 collective-permute-done.3
  193.7 5.8 collective-permute-start.5
  199.5 1.8 collective-permute-done.5
  201.3 5.9 collective-permute-start.7
  207.4 1.7 collective-permute-done.7
  209.1 5.9 collective-permute-start.9
  215.3 1.6 collective-permute-done.9
  216.9 5.9 collective-permute-start.11
  223.1 1.6 collective-permute-done.11
  224.6 5.9 collective-permute-start.13
  231.4 7.7 collective-permute-done.12
  239.2 7.7 collective-permute-done.14
  249.9 1.2 convolution_convert_fusion.3
  253.7 1.3 convert_element_type.213
  255.9 2.3 all_gather.54
  258.2 1.3 log_add_fusion
  262.2 2.4 all_gather.50
  264.7 63.0 %all-gather.6.cloned.1.call-done = bf16[896,2432]{1,0:T(8,128)(2,1)} async-done(((bf16[56,2432]{1,0:T(8,128)(2,1)}), bf16[896,2432]{1,0:T(8,128)(2,1)}) %all-gather.6.cloned.1.call-update) | async-done | bytes 4358160 | tf_op jit(solution)/shard_map/all_gather | solution.py:95
  327.7 5.3 fusion.77
  333.1 73.3 %all-gather.4.cloned.1.call-done = bf16[896,2432]{1,0:T(8,128)(2,1)} async-done(((bf16[56,2432]{1,0:T(8,128)(2,1)}), bf16[896,2432]{1,0:T(8,128)(2,1)}) %all-gather.4.cloned.1.call-update) | async-done | bytes 4358160 | tf_op jit(solution)/shard_map/all_gather | solution.py:94
  406.4 5.3 fusion.76
  411.7 73.4 %all-gather.8.cloned.1.call-done = bf16[2432,896]{0,1:T(8,128)(2,1)} async-done(((bf16[2432,56]{0,1:T(8,128)(2,1)}), bf16[2432,896]{0,1:T(8,128)(2,1)}) %all-gather.8.cloned.1.call-update) | async-done | bytes 4358160 | tf_op jit(solution)/shard_map/all_gather | solution.py:96
  485.1 6.9 multiply_convert_fusion
  492.0 1.5 fusion.78
  493.5 4.6 fusion.7
  498.2 6.3 fusion.80
  504.5 4.8 fusion.79
  509.3 1.9 fusion.31
  511.2 1.4 multiply_convert_fusion.3
  512.7 2.4 all_gather.55
  519.5 1.3 fusion.6
  520.8 5.0 convolution_convert_fusion.2
  525.8 6.1 fusion.81
  532.0 19.7 %pad_maximum_fusion = f32[896,7296]{1,0:T(8,128)} fusion(f32[896,2432]{1,0:T(8,128)} %fusion.81, f32[896,2432]{1,0:T(8,128)} %fusion.80, f32[896,2432]{1,0:T(8,128)} %fusion.79), kind=kLoop, calls=%fused_computation | loop fusion | flops 13074432 | bytes 52297728 | tf_op jit(solution)/shard_map/concatenate | solution.py:238
  554.3 2.1 pad_maximum_fusion.1
  556.5 4.4 all-to-all-start
  562.8 107.0 %all-reduce.3 = (f32[896]{0:T(1024)S(1)}, f32[896]{0:T(1024)S(1)}) all-reduce(f32[896]{0:T(1024)S(1)} %get-tuple-element.37, f32[896]{0:T(1024)S(1)} %copy-done.39), channel_id=1, replica_groups=mesh['fsdp'=16,'tp'=2] {'fsdp','tp'}, use_global_device_ids=true, to_apply=%region_15.16 | all-reduce | flops 1792 | bytes 14336 | tf_op jit(solution)/shard_map/psum | solution.py:317
  671.1 2.2 fusion.27
  675.1 593.4 %all-reduce.7.cloned.1.call-done = f32[896,7296]{1,0:T(8,128)} async-done(((f32[896,7296]{1,0:T(8,128)}), f32[896,7296]{1,0:T(8,128)}) %all-reduce.7.cloned.1.call-update) | async-done | bytes 26148880
  1268.5 2.9 dynamic-slice_bitcast_fusion
  (215 shorter events, 30.9 us)
Async XLA Ops:
  8.0 138.9 %copy-start.36 = (bf16[448,56]{0,1:T(8,128)(2,1)S(1)}, bf16[448,56]{0,1:T(8,128)(2,1)}, u32[]{:S(2)}) copy-start(bf16[448,56]{0,1:T(8,128)(2,1)} %param.24) | copy-start | bytes 150532
  8.0 251.5 %reduce-scatter.5.cloned.1.call-start = ((), (), s32[]{:S(2)}) async-start(), calls=%async_computation.5 | async-start | bytes 688128 | tf_op jit(solution)/shard_map/reduce_scatter | solution.py:195
  8.1 180.8 %collective-permute-start.1 = (bf16[56,448]{1,0:T(8,128)(2,1)}, bf16[56,448]{1,0:T(8,128)(2,1)S(1)}, u32[]{:S(2)}, u32[]{:S(2)}) collective-permute-start(bf16[56,448]{1,0:T(8,128)(2,1)} %param.21), channel_id=1, source_target_pairs={{0,30},{2,0},{4,2},{6,4},{8,6},{10,8},{12,10},{14,12},{16,14},{18,... | collective-permute-start | bytes 150536 | tf_op jit(solution)/shard_map/ppermute | solution.py:26
  15.0 176.6 %collective-permute-start = (bf16[56,448]{1,0:T(8,128)(2,1)}, bf16[56,448]{1,0:T(8,128)(2,1)S(1)}, u32[]{:S(2)}, u32[]{:S(2)}) collective-permute-start(bf16[56,448]{1,0:T(8,128)(2,1)} %param.21), channel_id=1, source_target_pairs={{0,2},{2,4},{4,6},{6,8},{8,10},{10,12},{12,14},{14,16},{16,18},{18... | collective-permute-start | bytes 150536 | tf_op jit(solution)/shard_map/ppermute | solution.py:21
  15.1 172.7 %copy-start.44 = (f32[32]{0:T(128)}, f32[32]{0:T(128)S(1)}, u32[]{:S(2)}) copy-start(f32[32]{0:T(128)S(1)} %multiply_power_fusion) | copy-start | bytes 388
  15.1 172.7 %copy-start.40 = (f32[256]{0:T(256)}, f32[256]{0:T(256)S(1)}, u32[]{:S(2)}) copy-start(f32[256]{0:T(256)S(1)} %fusion.65) | copy-start | bytes 3076
  18.2 169.6 %copy-start.46 = (f32[128]{0:T(128)}, f32[128]{0:T(128)S(1)}, u32[]{:S(2)}) copy-start(f32[128]{0:T(128)S(1)} %add_rsqrt_fusion.1) | copy-start | bytes 1540
  64.9 75.9 %copy-start.28 = (f32[896]{0:T(1024)}, f32[896]{0:T(1024)S(1)}, u32[]{:S(2)}) copy-start(f32[896]{0:T(1024)S(1)} %convert_element_type.200) | copy-start | bytes 10756
  101.8 44.2 %copy-start.10 = (bf16[896,64]{1,0:T(8,128)(2,1)}, bf16[896,64]{1,0:T(8,128)(2,1)S(1)}, u32[]{:S(2)}) copy-start(bf16[896,64]{1,0:T(8,128)(2,1)S(1)} %all_gather.47) | copy-start | bytes 344068
  140.8 6.1 copy-start.12
  144.1 43.8 %copy-start.35 = (bf16[56,448]{1,0:T(8,128)(2,1)S(1)}, bf16[56,448]{1,0:T(8,128)(2,1)}, u32[]{:S(2)}) copy-start(bf16[56,448]{1,0:T(8,128)(2,1)} %param.21) | copy-start | bytes 150532
  146.1 101.3 %copy-start.21 = (f32[256,32]{0,1:T(8,128)}, f32[256,32]{0,1:T(8,128)S(1)}, u32[]{:S(2)}) copy-start(f32[256,32]{0,1:T(8,128)S(1)} %get-tuple-element.65) | copy-start | bytes 98308
  146.9 101.0 %copy-start.30 = (bf16[256,32]{0,1:T(8,128)(2,1)}, bf16[256,32]{0,1:T(8,128)(2,1)S(1)}, u32[]{:S(2)}) copy-start(bf16[256,32]{0,1:T(8,128)(2,1)S(1)} %get-tuple-element.61) | copy-start | bytes 49156
  188.8 4.9 collective-permute-start.3
  191.7 7.8 collective-permute-start.2
  193.7 7.6 collective-permute-start.5
  199.5 7.9 collective-permute-start.4
  201.3 7.8 collective-permute-start.7
  207.4 7.9 collective-permute-start.6
  207.4 40.5 %copy-start.32 = (bf16[256,32]{0,1:T(8,128)(2,1)S(1)}, bf16[256,32]{0,1:T(8,128)(2,1)}, u32[]{:S(2)}) copy-start(bf16[256,32]{0,1:T(8,128)(2,1)} %get-tuple-element.62) | copy-start | bytes 49156
  207.4 40.4 %copy-start.34 = (pred[256,256]{0,1:T(8,128)(4,1)S(1)}, pred[256,256]{0,1:T(8,128)(4,1)}, u32[]{:S(2)}) copy-start(pred[256,256]{0,1:T(8,128)(4,1)} %fusion.36) | copy-start | bytes 196612
  209.1 7.8 collective-permute-start.9
  215.2 7.8 collective-permute-start.8
  216.9 7.8 collective-permute-start.11
  223.0 8.3 collective-permute-start.10
  224.6 14.5 %collective-permute-start.13 = (bf16[56,448]{1,0:T(8,128)(2,1)S(1)}, bf16[56,448]{1,0:T(8,128)(2,1)S(1)}, u32[]{:S(2)}, u32[]{:S(2)}) collective-permute-start(bf16[56,448]{1,0:T(8,128)(2,1)S(1)} %collective-permute-done.11), channel_id=1, source_target_pairs={{0,30},{2,0},{4,2},{6,4},{8,6},{10,8},{12,10},{14,12},{16,14},{18,... | collective-permute-start | bytes 150536 | tf_op jit(solution)/shard_map/ppermute | solution.py:26
  231.3 7.8 collective-permute-start.12
  239.1 7.8 collective-permute-start.14
  249.9 9.6 copy-start
  251.2 76.5 %all-gather.6.cloned.1.call-start = ((), (), s32[]{:S(2)}) async-start(), calls=%async_computation.7 | async-start | bytes 4630528 | tf_op jit(solution)/shard_map/all_gather | solution.py:95
  251.8 154.6 %all-gather.4.cloned.1.call-start = ((), (), s32[]{:S(2)}) async-start(), calls=%async_computation.6 | async-start | bytes 4630528 | tf_op jit(solution)/shard_map/all_gather | solution.py:94
  252.4 232.7 %all-gather.8.cloned.1.call-start = ((), (), s32[]{:S(2)}) async-start(), calls=%async_computation.8 | async-start | bytes 4630528 | tf_op jit(solution)/shard_map/all_gather | solution.py:96
  253.0 256.3 %reduce-scatter.9.cloned.1.call-start = ((), (), s32[]{:S(2)}) async-start(), calls=%async_computation.10 | async-start | bytes 688128 | tf_op jit(solution)/shard_map/reduce_scatter | solution.py:229
  485.1 6.9 copy-start.50
  498.1 63.5 %reduce-scatter.11.cloned.1.call-start = ((), (), s32[]{:S(2)}) async-start(), calls=%async_computation.11 | async-start | bytes 688128 | tf_op jit(solution)/shard_map/reduce_scatter | solution.py:292
  498.2 6.3 copy-start.3
  498.2 6.3 copy-start.15
  520.8 150.3 %reduce-scatter.7.cloned.1.call-start = ((), (), s32[]{:S(2)}) async-start(), calls=%async_computation.9 | async-start | bytes 688128 | tf_op jit(solution)/shard_map/reduce_scatter | solution.py:212
  532.0 736.5 %all-reduce.7.cloned.1.call-start = ((), (), s32[]{:S(2)}) async-start(), calls=%async_computation.12 | async-start | bytes 52297728
  556.4 5.2 copy-start.47
  556.4 6.4 copy-start.39
  556.4 114.6 %copy-start.4 = (bf16[128,896]{1,0:T(8,128)(2,1)S(1)}, bf16[128,896]{1,0:T(8,128)(2,1)}, u32[]{:S(2)}) copy-start(bf16[128,896]{1,0:T(8,128)(2,1)} %reduce-scatter.5.cloned.1.call-done) | copy-start | bytes 688132
  556.4 114.6 %copy-start.8 = (bf16[128,896]{1,0:T(8,128)(2,1)S(1)}, bf16[128,896]{1,0:T(8,128)(2,1)}, u32[]{:S(2)}) copy-start(bf16[128,896]{1,0:T(8,128)(2,1)} %param.18) | copy-start | bytes 688132
  556.4 114.6 %copy-start.9 = (bf16[128,896]{1,0:T(8,128)(2,1)S(1)}, bf16[128,896]{1,0:T(8,128)(2,1)}, u32[]{:S(2)}) copy-start(bf16[128,896]{1,0:T(8,128)(2,1)} %reduce-scatter.9.cloned.1.call-done) | copy-start | bytes 688132
  556.5 114.6 %copy-start.27 = (f32[896]{0:T(1024)S(1)}, f32[896]{0:T(1024)}, u32[]{:S(2)}) copy-start(f32[896]{0:T(1024)} %convert_element_type.213) | copy-start | bytes 10756
  556.5 114.6 %copy-start.43 = (f32[128]{0:T(128)S(1)}, f32[128]{0:T(128)}, u32[]{:S(2)}) copy-start(f32[128]{0:T(128)} %copy-done.42) | copy-start | bytes 1540
  556.5 114.6 %copy-start.49 = (f32[128]{0:T(128)S(1)}, f32[128]{0:T(128)}, u32[]{:S(2)}) copy-start(f32[128]{0:T(128)} %copy-done.48) | copy-start | bytes 1540
  556.5 116.8 %all-to-all-start = ((bf16[16,56,1024]{2,1,0:T(8,128)(2,1)}), bf16[16,56,1024]{2,1,0:T(8,128)(2,1)S(1)}, u32[]{:S(2)}, u32[]{:S(2)}) async-start(bf16[16,56,1024]{2,1,0:T(8,128)(2,1)} %pad_maximum_fusion.1), calls=%async_computation.4 | async-start | bytes 3670016 | tf_op jit(solution)/shard_map/all_to_all | solution.py:41
  (27 other events, 40.9 us)
Sparse Core Ops, SparseCore 0:
  251.3 3.7 reduce-scatter.4
  498.2 6.4 reduce-scatter.8
  520.9 6.4 reduce-scatter.10
  532.1 7.1 reduce-scatter.6
Sparse Core Ops, SparseCore 1:
  254.7 72.9 all-gather.5
  330.6 75.7 all-gather.3
  409.3 75.7 all-gather.7
  551.8 716.6 all-reduce.6
